TPU v7x, 256 devices: a whole 4x4x8 slice. The times are simulated.
256 devices in a mesh: ha: 8 (over x, y_lo), wa: 32 (over z, y_hi, core).
Axes of the slice: x: 4, y: 4 (y_hi: 2, y_lo: 2; y = y_hi * 2 + y_lo), z: 8, core: 2. Of those that a mesh axis runs over, the one named last changes fastest.
Arguments:
- tokens: bfloat16 [4, 64, 256, 1536], P(None, 'ha', 'wa'), may hold values from -6 to 6
- shift: float32 [1536], replicated, may hold values from -3 to 3
- scale: float32 [1536], replicated, may hold values from -3 to 3
- gate: float32 [1536], replicated, may hold values from -4 to 4
- qkv_weight: bfloat16 [1536, 4608], P('wa'), may hold values from -0.17860863 to 0.17860863
- out_weight: bfloat16 [1536, 1536], P('wa'), may hold values from -0.15625 to 0.15625
- q_gain: float32 [128], replicated, may hold values from 1.4 to 6.5
- k_gain: float32 [128], replicated, may hold values from 1.4 to 6.5
Outputs:
- update: bfloat16 [4, 64, 256, 1536], P(None, 'ha', 'wa')
All inputs are finite; a program needn't handle non-finite values.
Results may differ from a plain program's by a relative error of at most 0.009.
The roundings to bfloat16 on the way count: a program that leaves them out, or rounds other values in their place, can miss the bound.
Values may be sent and summed in bfloat16 or wider, within the bound.
No kernel may reach another device: no remote copies, remote signals or barrier semaphores. Data moves between devices by JAX's collectives and lax.ppermute only.
A program may use at most 128 MiB of HBM per device.

v0:
```python
import jax
import jax.numpy as jnp
from jax import lax
from jax.sharding import PartitionSpec as P

HEADS = 12
HD = 128
TILE_T = 4


def padded(x, sides, width):
    for axis, dim in sides:
        peers, length = (lax.axis_size(axis), x.shape[dim])
        up = [(i, (i + 1) % peers) for i in range(peers - 1)]
        down = [(j, i) for i, j in up]
        last = lax.slice_in_dim(x, length - width, length, axis=dim)
        initial = lax.slice_in_dim(x, 0, width, axis=dim)
        before = lax.ppermute(last, axis, up)
        after = lax.ppermute(initial, axis, down)
        x = jnp.concatenate([before, x, after], axis=dim)
    return x


def add_rows(left, piece):
    return jnp.dot(left, piece, preferred_element_type=jnp.float32)


def per_head_norm(raw, gain):
    return (raw * lax.rsqrt(jnp.mean(raw * raw, axis=-1, keepdims=True) + 1e-06) * gain).astype(
        jnp.bfloat16
    )


def shards(tokens, shift, scale, gate, qkv_weight, out_weight, q_gain, k_gain):
    frame_list, tile_h, tile_w, width = tokens.shape
    count = frame_list * tile_h * tile_w
    inner = HEADS * HD
    groups = frame_list // TILE_T
    tall = lax.axis_size("ha")
    wide = lax.axis_size("wa")
    flat = tokens.reshape(count, width).astype(jnp.float32)
    mean = jnp.mean(flat, axis=-1, keepdims=True)
    centred = flat - mean
    var = jnp.mean(centred * centred, axis=-1, keepdims=True)
    normed = centred / jnp.sqrt(var + 1e-06)
    modulated = (normed * (1.0 + scale) + shift).astype(jnp.bfloat16)
    projected = add_rows(modulated, lax.all_gather(qkv_weight, "wa", axis=0, tiled=True))
    query = per_head_norm(projected[:, :inner].reshape(count, HEADS, HD), q_gain)
    key = per_head_norm(projected[:, inner : 2 * inner].reshape(count, HEADS, HD), k_gain)
    value = projected[:, 2 * inner :].astype(jnp.bfloat16)
    both = jnp.concatenate(
        [
            key.reshape(frame_list, tile_h, tile_w, inner),
            value.reshape(frame_list, tile_h, tile_w, inner),
        ],
        axis=-1,
    )
    window = padded(both, (("ha", 1), ("wa", 2)), tile_h)
    rows = lax.axis_index("ha") * tile_h - tile_h + jnp.arange(3 * tile_h, dtype=jnp.int32)
    cols = lax.axis_index("wa") * tile_w - tile_w + jnp.arange(3 * tile_w, dtype=jnp.int32)
    rows_ok = (rows >= 0) & (rows < tile_h * tall)
    cols_ok = (cols >= 0) & (cols < tile_w * wide)
    valid = jnp.broadcast_to(
        rows_ok[:, None] & cols_ok[None, :], (TILE_T, 3 * tile_h, 3 * tile_w)
    ).reshape(-1)
    window = window.reshape(groups, -1, 2 * inner)
    keys = window[:, :, :inner].reshape(groups, -1, HEADS, HD)
    values = window[:, :, inner:].reshape(groups, -1, HEADS, HD)
    queries = query.reshape(groups, -1, HEADS, HD)
    inv_root = 1.0 / jnp.sqrt(jnp.float32(HD))

    def one_head(head):
        query_head_rows = lax.dynamic_index_in_dim(queries, head, 2, keepdims=False)
        key_head_rows = lax.dynamic_index_in_dim(keys, head, 2, keepdims=False)
        value_head_rows = lax.dynamic_index_in_dim(values, head, 2, keepdims=False)
        scores = (
            jnp.einsum(
                "nur,ncr->nuc", query_head_rows, key_head_rows, preferred_element_type=jnp.float32
            )
            * inv_root
        )
        scores = jnp.where(valid[None, None, :], scores, -jnp.inf)
        top = jnp.max(scores, axis=-1, keepdims=True)
        expo = jnp.exp(scores - top)
        total = jnp.sum(expo, axis=-1, keepdims=True)
        probability_rows = expo.astype(jnp.bfloat16)
        summed_output = jnp.einsum(
            "ypi,yif->ypf", probability_rows, value_head_rows, preferred_element_type=jnp.float32
        )
        return summed_output / total

    per_head = lax.map(one_head, jnp.arange(HEADS, dtype=jnp.int32))
    attended = jnp.transpose(per_head, (1, 2, 0, 3)).reshape(count, inner).astype(jnp.bfloat16)
    output = add_rows(attended, lax.all_gather(out_weight, "wa", axis=0, tiled=True))
    return (gate * output).astype(jnp.bfloat16).reshape(frame_list, tile_h, tile_w, width)


def solution(mesh):
    return jax.shard_map(
        shards,
        mesh=mesh,
        in_specs=(P(None, "ha", "wa", None), P(), P(), P(), P("wa", None), P("wa", None), P(), P()),
        out_specs=P(None, "ha", "wa", None),
        check_vma=False,
    )
```

profile of v0, /device:TPU:28, one launch (start us, length us, event | category | flops | bytes accessed | tf_op | source)
XLA Modules:
  0.0 474.7 jit_solution(12902752711311697447)
XLA Ops:
  12.1 123.9 %all-gather.3.cloned.1.call-done = bf16[1536,4608]{1,0:T(8,128)(2,1)} async-done(((bf16[48,4608]{1,0:T(8,128)(2,1)}), bf16[1536,4608]{1,0:T(8,128)(2,1)}) %all-gather.3.cloned.1.call-update) | async-done | bytes 14155792 | tf_op jit(solution)/shard_map/all_gather | solution.py:47
  136.0 7.0 %fusion.29 = f32[256,4608]{1,0:T(8,128)S(1)} fusion(bf16[256,1536]{1,0:T(8,128)(2,1)S(1)} %fusion.26, bf16[1536,4608]{1,0:T(8,128)(2,1)} %all-gather.3.cloned.1.call-done), kind=kOutput, calls=%fused_computation.47 | convolution fusion | flops 3623878656 | bytes 19660800 | tf_op jit(solution)/shard_map/dot_general | solution.py:25
  143.1 2.5 slice_multiply_fusion
  150.9 2.2 multiply_convert_fusion
  153.3 1.9 collective-permute-start.1
  155.2 4.8 %collective-permute-start = (bf16[4,8,8,3072]{3,2,1,0:T(8,128)(2,1)S(1)}, bf16[4,8,8,3072]{3,2,1,0:T(8,128)(2,1)S(1)}, u32[]{:S(2)}, u32[]{:S(2)}) collective-permute-start(bf16[4,8,8,3072]{3,2,1,0:T(8,128)(2,1)S(1)} %pad_maximum_fusion.2), channel_id=1, source_target_pairs={{0,32},{32,64},{64,96},{96,128},{128,160},{160,192},{192,224},{1,3... | collective-permute-start | bytes 4718600 | tf_op jit(solution)/shard_map/ppermute | solution.py:18
  160.1 63.2 %collective-permute-done.1 = bf16[4,8,8,3072]{3,2,1,0:T(8,128)(2,1)S(1)} collective-permute-done((bf16[4,8,8,3072]{3,2,1,0:T(8,128)(2,1)S(1)}, bf16[4,8,8,3072]{3,2,1,0:T(8,128)(2,1)S(1)}, u32[]{:S(2)}, u32[]{:S(2)}) %collective-permute-start.1) | collective-permute-done | bytes 1572896 | tf_op jit(solution)/shard_map/ppermute | solution.py:19
  223.3 3.1 collective-permute-done
  226.4 2.7 pad_maximum_fusion.1
  229.1 3.6 collective-permute-start.3
  232.7 1.9 collective-permute-start.2
  234.8 3.0 copy.9
  237.8 3.0 copy.10
  242.4 2.7 multiply_convert_fusion.1
  245.1 41.1 %collective-permute-done.3 = bf16[4,24,8,3072]{3,2,1,0:T(8,128)(2,1)} collective-permute-done((bf16[4,24,8,3072]{3,2,1,0:T(8,128)(2,1)}, bf16[4,24,8,3072]{3,2,1,0:T(8,128)(2,1)}, u32[]{:S(2)}, u32[]{:S(2)}) %collective-permute-start.3) | collective-permute-done | bytes 4718624 | tf_op jit(solution)/shard_map/ppermute | solution.py:19
  286.2 66.0 %collective-permute-done.2 = bf16[4,24,8,3072]{3,2,1,0:T(8,128)(2,1)} collective-permute-done((bf16[4,24,8,3072]{3,2,1,0:T(8,128)(2,1)}, bf16[4,24,8,3072]{3,2,1,0:T(8,128)(2,1)}, u32[]{:S(2)}, u32[]{:S(2)}) %collective-permute-start.2) | collective-permute-done | bytes 4718624 | tf_op jit(solution)/shard_map/ppermute | solution.py:18
  352.2 6.8 %pad_maximum_fusion = bf16[4,24,24,3072]{3,2,1,0:T(8,128)(2,1)S(1)} fusion(bf16[4,24,8,3072]{3,2,1,0:T(8,128)(2,1)} %collective-permute-done.3, bf16[4,8,8,3072]{3,2,1,0:T(8,128)(2,1)S(1)} %collective-permute-done.1, bf16[4,8,8,1536]{3,2,1,0:T(8,128)(2,1)S(1)} %bitcast.62, bf16[4,8,8,1536]{3,2,1,0:T(8,128)(2,1)S(1)} %multiply_convert_fusion, ...), kind=kLoop, calls=%fused_computation.19 | loop fusion | flops 84934656 | bytes 28311552 | tf_op jit(solution)/shard_map/concatenate | solution.py:20
  359.0 5.4 %fusion.28 = (bf16[1,2304,1536]{2,1,0:T(8,128)(2,1)}, bf16[1,2304,1536]{2,1,0:T(8,128)(2,1)}) fusion(bf16[1,2304,3072]{2,1,0:T(8,128)(2,1)S(1)} %bitcast.57), kind=kLoop, calls=%fused_computation.46 | loop fusion | bytes 28311552 | tf_op jit(solution)/shard_map/slice | solution.py:68
  364.4 10.2 %copy.24 = bf16[1,2304,1536]{1,2,0:T(8,128)(2,1)} copy(bf16[1,2304,1536]{2,1,0:T(8,128)(2,1)} %get-tuple-element.84) | data formatting | bytes 14155776
  374.5 9.9 %copy.25 = bf16[1,2304,1536]{1,2,0:T(8,128)(2,1)} copy(bf16[1,2304,1536]{2,1,0:T(8,128)(2,1)} %get-tuple-element.83) | data formatting | bytes 14155776
  384.5 78.7 %while.11 = (s32[]{:T(128)}, bf16[12,1,256,128]{2,3,0,1:T(8,128)(2,1)S(1)}, s32[12]{0:T(128)S(1)}, bf16[1,256,12,128]{1,3,2,0:T(8,128)(2,1)}, bf16[1,2304,12,128...) while((s32[]{:T(128)}, ...), condition=%wide.region_7.8_spmd.clone, body=%wide.region_4.7_spmd.clone.sunk | while | flops 306183680 | bytes 8666851 | solution.py:92
  400.3 1.7 fusion.41
  413.4 1.7 fusion.41
  463.3 4.6 fusion.22
  (138 shorter events, 64.2 us)
Async XLA Ops:
  6.5 3.8 copy-start
  6.5 4.5 copy-start.2
  6.5 129.5 %all-gather.3.cloned.1.call-start = ((), (), s32[]{:S(2)}) async-start(), calls=%async_computation | async-start | bytes 14598144 | tf_op jit(solution)/shard_map/all_gather | solution.py:47
  7.3 456.0 %all-gather.5.cloned.1.call-start = ((), (), s32[]{:S(2)}) async-start(), calls=%async_computation.1 | async-start | bytes 4866048 | tf_op jit(solution)/shard_map/all_gather | solution.py:94
  153.3 70.0 %collective-permute-start.1 = (bf16[4,8,8,3072]{3,2,1,0:T(8,128)(2,1)S(1)}, bf16[4,8,8,3072]{3,2,1,0:T(8,128)(2,1)S(1)}, u32[]{:S(2)}, u32[]{:S(2)}) collective-permute-start(bf16[4,8,8,3072]{3,2,1,0:T(8,128)(2,1)S(1)} %pad_maximum_fusion.2), channel_id=1, source_target_pairs={{32,0},{64,32},{96,64},{128,96},{160,128},{192,160},{224,192},{33,... | collective-permute-start | bytes 4718600 | tf_op jit(solution)/shard_map/ppermute | solution.py:19
  155.2 71.1 %collective-permute-start = (bf16[4,8,8,3072]{3,2,1,0:T(8,128)(2,1)S(1)}, bf16[4,8,8,3072]{3,2,1,0:T(8,128)(2,1)S(1)}, u32[]{:S(2)}, u32[]{:S(2)}) collective-permute-start(bf16[4,8,8,3072]{3,2,1,0:T(8,128)(2,1)S(1)} %pad_maximum_fusion.2), channel_id=1, source_target_pairs={{0,32},{32,64},{64,96},{96,128},{128,160},{160,192},{192,224},{1,3... | collective-permute-start | bytes 4718600 | tf_op jit(solution)/shard_map/ppermute | solution.py:18
  226.4 2.7 copy-start.3
  229.1 57.2 %collective-permute-start.3 = (bf16[4,24,8,3072]{3,2,1,0:T(8,128)(2,1)}, bf16[4,24,8,3072]{3,2,1,0:T(8,128)(2,1)}, u32[]{:S(2)}, u32[]{:S(2)}) collective-permute-start(bf16[4,24,8,3072]{3,2,1,0:T(8,128)(2,1)} %pad_maximum_fusion.1), channel_id=1, source_target_pairs={{1,0},{2,1},{3,2},{4,3},{5,4},{6,5},{7,6},{8,7},{9,8},{10,9},{11,1... | collective-permute-start | bytes 14155784 | tf_op jit(solution)/shard_map/ppermute | solution.py:19
  232.7 119.5 %collective-permute-start.2 = (bf16[4,24,8,3072]{3,2,1,0:T(8,128)(2,1)}, bf16[4,24,8,3072]{3,2,1,0:T(8,128)(2,1)}, u32[]{:S(2)}, u32[]{:S(2)}) collective-permute-start(bf16[4,24,8,3072]{3,2,1,0:T(8,128)(2,1)} %pad_maximum_fusion.1), channel_id=1, source_target_pairs={{0,1},{1,2},{2,3},{3,4},{4,5},{5,6},{6,7},{7,8},{8,9},{9,10},{10,1... | collective-permute-start | bytes 14155784 | tf_op jit(solution)/shard_map/ppermute | solution.py:18
  237.8 4.6 copy-start.5
  242.4 109.9 %copy-start.4 = (bf16[4,8,8,3072]{3,2,1,0:T(8,128)(2,1)S(1)}, bf16[4,8,8,3072]{3,2,1,0:T(8,128)(2,1)}, u32[]{:S(2)}) copy-start(bf16[4,8,8,3072]{3,2,1,0:T(8,128)(2,1)} %copy-done.3) | copy-start | bytes 4718596
  374.5 10.0 %copy-start.6 = (bf16[12,1,256,128]{2,3,0,1:T(8,128)(2,1)S(1)}, bf16[12,1,256,128]{2,3,0,1:T(8,128)(2,1)}, u32[]{:S(2)}) copy-start(bf16[12,1,256,128]{2,3,0,1:T(8,128)(2,1)} %custom-call) | copy-start | bytes 2359300
  384.5 78.8 %copy-start.7 = (f32[1536]{0:T(1024)S(1)}, f32[1536]{0:T(1024)}, u32[]{:S(2)}) copy-start(f32[1536]{0:T(1024)} %param.13) | copy-start | bytes 18436
  463.3 4.6 copy-start.1
Sparse Core Ops, SparseCore 0:
  10.1 125.8 all-gather.2
  234.8 133.5 all-gather.4
where the time goes:
time: 477 us; the launch traced here: 475 us
  waiting for transfers between devices  298 us (62%)
  matrix products  51.1 us (11%)
  local copies, waits for them, and re-layouts  45.3 us (9%)
  other arithmetic  30.5 us (6%)
  loops' own time  23.9 us (5%)
  between operations  13.6 us (3%)
  starting transfers between devices  12.3 us (3%)
    all_gather x1, waiting for transfers between devices, shards(): lax.all_gather(qkv_weight, 'wa', axis=0, tiled=True)  124 us
    ppermute x2, waiting for transfers between devices, padded(): after = lax.ppermute(initial, axis, down)  104 us
    ppermute x2, waiting for transfers between devices, padded(): before = lax.ppermute(last, axis, up)  69.1 us
    another operation x1, loops' own time, shards(): per_head = lax.map(one_head, jnp.arange(HEADS, dtype=jnp.int32))  23.9 us
    dot_general x12, matrix products, one_head(): jnp.einsum('nur,ncr->nuc', query_head_rows, key_head_rows, preferred_elem...  20.3 us
    unnamed x18, local copies, waits for them, and re-layouts  20.1 us
    dot_general x12, matrix products, one_head(): jnp.einsum('ypi,yif->ypf', probability_rows, value_head_rows, preferred_e...  19.1 us
    dot_general x2, matrix products, add_rows(): return jnp.dot(left, piece, preferred_element_type=jnp.float32)  11.7 us
  transfers between devices with their start and end apart: 6, of which 5 were waited for; matrix products, arithmetic and copies ran while one was open for 22% of the time, Pallas kernels for 0%

commit v1 on v0

--- a/solution.py
+++ b/solution.py
@@ -44,7 +44,12 @@
     var = jnp.mean(centred * centred, axis=-1, keepdims=True)
     normed = centred / jnp.sqrt(var + 1e-06)
     modulated = (normed * (1.0 + scale) + shift).astype(jnp.bfloat16)
-    projected = add_rows(modulated, lax.all_gather(qkv_weight, "wa", axis=0, tiled=True))
+    projected = add_rows(
+        modulated,
+        jnp.concatenate(
+            lax.all_to_all(jnp.stack([qkv_weight] * lax.axis_size("wa")), "wa", 0, 0), axis=0
+        ),
+    )
     query = per_head_norm(projected[:, :inner].reshape(count, HEADS, HD), q_gain)
     key = per_head_norm(projected[:, inner : 2 * inner].reshape(count, HEADS, HD), k_gain)
     value = projected[:, 2 * inner :].astype(jnp.bfloat16)

time: 477 us -> 676 us (1.42)
  waiting for transfers between devices: 298 us -> 479 us
  starting transfers between devices: 12.3 us -> 23 us
  local copies, waits for them, and re-layouts: 45.3 us -> 52.8 us
    all_to_all x0 -> x1, waiting for transfers between devices: none -> 304 us  [shards(): lax.all_to_all(jnp.stack([qkv_weight] * lax.axis_size('wa')), 'wa', 0, 0)]
    all_gather x1 -> x0, waiting for transfers between devices: 124 us -> none  [shards(): lax.all_gather(qkv_weight, 'wa', axis=0, tiled=True)]
    all_to_all x0 -> x1, starting transfers between devices: none -> 11.8 us  [shards(): lax.all_to_all(jnp.stack([qkv_weight] * lax.axis_size('wa')), 'wa', 0, 0)]
    another operation x0 -> x1, local copies, waits for them, and re-layouts: none -> 7.75 us  [shards(): jnp.stack([qkv_weight] * lax.axis_size('wa'))]
    unnamed x18 -> x22, local copies, waits for them, and re-layouts: 20.1 us -> 20.1 us
  transfers between devices with their start and end apart: 6 -> 6, of which waited for: 5 -> 5; matrix products, arithmetic and copies ran while one was open for 22% -> 15% of each run, Pallas kernels for 0% -> 0%
where the time goes in v1:
time: 676 us; the launch traced here: 670 us
  waiting for transfers between devices  479 us (71%)
  local copies, waits for them, and re-layouts  52.8 us (8%)
  matrix products  51.1 us (8%)
  other arithmetic  26.9 us (4%)
  loops' own time  23.9 us (4%)
  starting transfers between devices  23 us (3%)
  between operations  13.6 us (2%)
    all_to_all x1, waiting for transfers between devices, shards(): lax.all_to_all(jnp.stack([qkv_weight] * lax.axis_size('wa')), 'wa', 0, 0)  304 us
    ppermute x2, waiting for transfers between devices, padded(): after = lax.ppermute(initial, axis, down)  104 us
    ppermute x2, waiting for transfers between devices, padded(): before = lax.ppermute(last, axis, up)  71.2 us
    another operation x1, loops' own time, shards(): per_head = lax.map(one_head, jnp.arange(HEADS, dtype=jnp.int32))  23.9 us
    dot_general x12, matrix products, one_head(): jnp.einsum('nur,ncr->nuc', query_head_rows, key_head_rows, preferred_elem...  20.4 us
    unnamed x22, local copies, waits for them, and re-layouts  20.1 us
    dot_general x12, matrix products, one_head(): jnp.einsum('ypi,yif->ypf', probability_rows, value_head_rows, preferred_e...  19.1 us
  transfers between devices with their start and end apart: 6, of which 5 were waited for; matrix products, arithmetic and copies ran while one was open for 15% of the time, Pallas kernels for 0%

profile of v1, /device:TPU:28, one launch (start us, length us, event | category | flops | bytes accessed | tf_op | source)
XLA Modules:
  0.0 670.4 jit_solution(3884243082450404027)
XLA Ops:
  6.5 7.8 %stack.2 = bf16[32,48,4608]{2,1,0:T(8,128)(2,1)} broadcast(bf16[48,4608]{1,0:T(8,128)(2,1)} %param.14), dimensions={1,2} | broadcast | bytes 14598144 | tf_op jit(solution)/shard_map/stack | solution.py:50
  14.3 11.8 %all-to-all-start = ((bf16[32,48,4608]{2,1,0:T(8,128)(2,1)}), bf16[32,48,4608]{2,1,0:T(8,128)(2,1)}, u32[]{:S(2)}, u32[]{:S(2)}) async-start(bf16[32,48,4608]{2,1,0:T(8,128)(2,1)} %stack.2), calls=%async_computation | async-start | bytes 28311552 | tf_op jit(solution)/shard_map/all_to_all | solution.py:50
  27.1 304.0 %all-to-all-done = bf16[32,48,4608]{2,1,0:T(8,128)(2,1)} async-done(((bf16[32,48,4608]{2,1,0:T(8,128)(2,1)}), bf16[32,48,4608]{2,1,0:T(8,128)(2,1)}, u32[]{:S(2)}, u32[]{:S(2)}) %all-to-all-start) | async-done | bytes 14155808 | tf_op jit(solution)/shard_map/all_to_all | solution.py:50
  331.1 7.0 %fusion.31 = f32[256,4608]{1,0:T(8,128)S(1)} fusion(bf16[256,1536]{1,0:T(8,128)(2,1)S(1)} %bitcast.59, bf16[1536,4608]{1,0:T(8,128)(2,1)} %bitcast.1), kind=kOutput, calls=%fused_computation.48 | convolution fusion | flops 3623878656 | bytes 19660800 | tf_op jit(solution)/shard_map/dot_general | solution.py:25
  338.1 2.5 slice_multiply_fusion
  346.0 2.2 multiply_convert_fusion
  348.4 2.7 collective-permute-start.1
  351.0 4.1 collective-permute-start
  355.1 63.4 %collective-permute-done.1 = bf16[4,8,8,3072]{3,2,1,0:T(8,128)(2,1)S(1)} collective-permute-done((bf16[4,8,8,3072]{3,2,1,0:T(8,128)(2,1)S(1)}, bf16[4,8,8,3072]{3,2,1,0:T(8,128)(2,1)S(1)}, u32[]{:S(2)}, u32[]{:S(2)}) %collective-permute-start.1) | collective-permute-done | bytes 1572896 | tf_op jit(solution)/shard_map/ppermute | solution.py:19
  418.5 2.6 collective-permute-done
  421.2 2.7 pad_maximum_fusion.1
  423.9 1.9 collective-permute-start.3
  425.8 2.6 collective-permute-start.2
  428.5 3.0 copy.9
  431.6 3.0 copy.10
  436.2 2.7 multiply_convert_fusion.1
  438.9 40.4 %collective-permute-done.3 = bf16[4,24,8,3072]{3,2,1,0:T(8,128)(2,1)} collective-permute-done((bf16[4,24,8,3072]{3,2,1,0:T(8,128)(2,1)}, bf16[4,24,8,3072]{3,2,1,0:T(8,128)(2,1)}, u32[]{:S(2)}, u32[]{:S(2)}) %collective-permute-start.3) | collective-permute-done | bytes 4718624 | tf_op jit(solution)/shard_map/ppermute | solution.py:19
  479.3 68.5 %collective-permute-done.2 = bf16[4,24,8,3072]{3,2,1,0:T(8,128)(2,1)} collective-permute-done((bf16[4,24,8,3072]{3,2,1,0:T(8,128)(2,1)}, bf16[4,24,8,3072]{3,2,1,0:T(8,128)(2,1)}, u32[]{:S(2)}, u32[]{:S(2)}) %collective-permute-start.2) | collective-permute-done | bytes 4718624 | tf_op jit(solution)/shard_map/ppermute | solution.py:18
  547.9 6.9 %pad_maximum_fusion = bf16[4,24,24,3072]{3,2,1,0:T(8,128)(2,1)S(1)} fusion(bf16[4,24,8,3072]{3,2,1,0:T(8,128)(2,1)} %collective-permute-done.3, bf16[4,8,8,3072]{3,2,1,0:T(8,128)(2,1)S(1)} %collective-permute-done.1, bf16[4,8,8,1536]{3,2,1,0:T(8,128)(2,1)S(1)} %bitcast.54, bf16[4,8,8,1536]{3,2,1,0:T(8,128)(2,1)S(1)} %multiply_convert_fusion, ...), kind=kLoop, calls=%fused_computation.19 | loop fusion | flops 84934656 | bytes 28311552 | tf_op jit(solution)/shard_map/concatenate | solution.py:20
  554.7 5.4 fusion.30
  560.2 9.7 %copy.24 = bf16[1,2304,1536]{1,2,0:T(8,128)(2,1)} copy(bf16[1,2304,1536]{2,1,0:T(8,128)(2,1)} %get-tuple-element.84) | data formatting | bytes 14155776
  569.9 10.3 %copy.25 = bf16[1,2304,1536]{1,2,0:T(8,128)(2,1)} copy(bf16[1,2304,1536]{2,1,0:T(8,128)(2,1)} %get-tuple-element.83) | data formatting | bytes 14155776
  580.2 78.7 %while.11 = (s32[]{:T(128)}, bf16[12,1,256,128]{2,3,0,1:T(8,128)(2,1)S(1)}, s32[12]{0:T(128)S(1)}, bf16[1,256,12,128]{1,3,2,0:T(8,128)(2,1)}, bf16[1,2304,12,128...) while((s32[]{:T(128)}, ...), condition=%wide.region_7.8_spmd.clone, body=%wide.region_4.7_spmd.clone.sunk | while | flops 306183680 | bytes 8666851 | solution.py:97
  659.0 4.6 fusion.22
  (140 shorter events, 63.0 us)
Async XLA Ops:
  6.5 20.1 %copy-start = (f32[128]{0:T(128)S(1)}, f32[128]{0:T(128)}, u32[]{:S(2)}) copy-start(f32[128]{0:T(128)} %param.17) | copy-start | bytes 1540
  14.3 11.8 %copy-start.2 = (bf16[4,8,8,1536]{3,2,1,0:T(8,128)(2,1)S(1)}, bf16[4,8,8,1536]{3,2,1,0:T(8,128)(2,1)}, u32[]{:S(2)}) copy-start(bf16[4,8,8,1536]{3,2,1,0:T(8,128)(2,1)} %param.10) | copy-start | bytes 2359300
  14.3 12.4 %copy-start.6 = (f32[1536]{0:T(1024)S(1)}, f32[1536]{0:T(1024)}, u32[]{:S(2)}) copy-start(f32[1536]{0:T(1024)} %param.12) | copy-start | bytes 18436
  14.3 12.4 %copy-start.5 = (f32[1536]{0:T(1024)S(1)}, f32[1536]{0:T(1024)}, u32[]{:S(2)}) copy-start(f32[1536]{0:T(1024)} %param.11) | copy-start | bytes 18436
  14.3 316.8 %all-to-all-start = ((bf16[32,48,4608]{2,1,0:T(8,128)(2,1)}), bf16[32,48,4608]{2,1,0:T(8,128)(2,1)}, u32[]{:S(2)}, u32[]{:S(2)}) async-start(bf16[32,48,4608]{2,1,0:T(8,128)(2,1)} %stack.2), calls=%async_computation | async-start | bytes 28311552 | tf_op jit(solution)/shard_map/all_to_all | solution.py:50
  26.1 632.9 %all-gather.2.cloned.1.call-start = ((), (), s32[]{:S(2)}) async-start(), calls=%async_computation.1 | async-start | bytes 4866048 | tf_op jit(solution)/shard_map/all_gather | solution.py:99
  348.4 70.2 %collective-permute-start.1 = (bf16[4,8,8,3072]{3,2,1,0:T(8,128)(2,1)S(1)}, bf16[4,8,8,3072]{3,2,1,0:T(8,128)(2,1)S(1)}, u32[]{:S(2)}, u32[]{:S(2)}) collective-permute-start(bf16[4,8,8,3072]{3,2,1,0:T(8,128)(2,1)S(1)} %pad_maximum_fusion.2), channel_id=1, source_target_pairs={{32,0},{64,32},{96,64},{128,96},{160,128},{192,160},{224,192},{33,... | collective-permute-start | bytes 4718600 | tf_op jit(solution)/shard_map/ppermute | solution.py:19
  351.0 70.2 %collective-permute-start = (bf16[4,8,8,3072]{3,2,1,0:T(8,128)(2,1)S(1)}, bf16[4,8,8,3072]{3,2,1,0:T(8,128)(2,1)S(1)}, u32[]{:S(2)}, u32[]{:S(2)}) collective-permute-start(bf16[4,8,8,3072]{3,2,1,0:T(8,128)(2,1)S(1)} %pad_maximum_fusion.2), channel_id=1, source_target_pairs={{0,32},{32,64},{64,96},{96,128},{128,160},{160,192},{192,224},{1,3... | collective-permute-start | bytes 4718600 | tf_op jit(solution)/shard_map/ppermute | solution.py:18
  421.2 2.7 copy-start.3
  423.9 55.4 %collective-permute-start.3 = (bf16[4,24,8,3072]{3,2,1,0:T(8,128)(2,1)}, bf16[4,24,8,3072]{3,2,1,0:T(8,128)(2,1)}, u32[]{:S(2)}, u32[]{:S(2)}) collective-permute-start(bf16[4,24,8,3072]{3,2,1,0:T(8,128)(2,1)} %pad_maximum_fusion.1), channel_id=1, source_target_pairs={{1,0},{2,1},{3,2},{4,3},{5,4},{6,5},{7,6},{8,7},{9,8},{10,9},{11,1... | collective-permute-start | bytes 14155784 | tf_op jit(solution)/shard_map/ppermute | solution.py:19
  425.8 122.0 %collective-permute-start.2 = (bf16[4,24,8,3072]{3,2,1,0:T(8,128)(2,1)}, bf16[4,24,8,3072]{3,2,1,0:T(8,128)(2,1)}, u32[]{:S(2)}, u32[]{:S(2)}) collective-permute-start(bf16[4,24,8,3072]{3,2,1,0:T(8,128)(2,1)} %pad_maximum_fusion.1), channel_id=1, source_target_pairs={{0,1},{1,2},{2,3},{3,4},{4,5},{5,6},{6,7},{7,8},{8,9},{9,10},{10,1... | collective-permute-start | bytes 14155784 | tf_op jit(solution)/shard_map/ppermute | solution.py:18
  431.6 4.6 copy-start.7
  436.1 111.7 %copy-start.4 = (bf16[4,8,8,3072]{3,2,1,0:T(8,128)(2,1)S(1)}, bf16[4,8,8,3072]{3,2,1,0:T(8,128)(2,1)}, u32[]{:S(2)}) copy-start(bf16[4,8,8,3072]{3,2,1,0:T(8,128)(2,1)} %copy-done.3) | copy-start | bytes 4718596
  569.8 10.3 %copy-start.8 = (bf16[12,1,256,128]{2,3,0,1:T(8,128)(2,1)S(1)}, bf16[12,1,256,128]{2,3,0,1:T(8,128)(2,1)}, u32[]{:S(2)}) copy-start(bf16[12,1,256,128]{2,3,0,1:T(8,128)(2,1)} %custom-call) | copy-start | bytes 2359300
  580.2 78.8 %copy-start.9 = (f32[1536]{0:T(1024)S(1)}, f32[1536]{0:T(1024)}, u32[]{:S(2)}) copy-start(f32[1536]{0:T(1024)} %param.13) | copy-start | bytes 18436
  659.0 4.6 copy-start.1
Sparse Core Ops, SparseCore 0:
  428.6 137.5 all-gather.1
